TPU v7x, 32 devices: a whole 2x2x4 slice. The times are simulated.
32 devices in a mesh: frame: 8 (over y, x, core), head: 4 (over z).
Axes of the slice: x: 2, y: 2, z: 4, core: 2. Of those that a mesh axis runs over, the one named last changes fastest.
Arguments:
- queries: bfloat16 [4, 2048, 4096], P(None, 'frame', 'head'), may hold values from -6 to 6
- keys: bfloat16 [4, 2048, 4096], P(None, 'frame', 'head'), may hold values from -6 to 6
- values: bfloat16 [4, 2048, 4096], P(None, 'frame', 'head'), may hold values from -6 to 6
- step_sizes: bfloat16 [4, 2048, 16], P(None, 'frame', 'head'), may hold values from 9e-05 to 1.25, as said below
- starts: int32 [4], replicated, may hold values from 0 to 7, as said below
- resets: int32 [4, 8], replicated, may hold values 0 or 1
- init_in: bfloat16 [16, 256, 1024], P('head'), may hold values from -0.375 to 0.375
- init_out: bfloat16 [16, 512, 256], P('head'), may hold values from -0.25 to 0.25
- gain: float32 [4096], P('head'), may hold values from 0.25 to 1.75
- out_proj: bfloat16 [4096, 5120], P('head'), may hold values from -0.125 to 0.125
Outputs:
- mixed_out: bfloat16 [4, 2048, 5120], P(None, 'frame', 'head')
Inputs may be any that keep to these rules, and one draw needn't show every extreme that they name: `starts`: 4 distinct blocks. `step_sizes`: positive.
All inputs are finite; a program needn't handle non-finite values.
Results may differ from a plain program's by a relative error of at most 0.035.
Values may be sent and summed in bfloat16 or wider, within the bound.
No kernel may reach another device: no remote copies, remote signals or barrier semaphores. Data moves between devices by JAX's collectives and lax.ppermute only.
A program may use at most 128 MiB of HBM per device.

v0:
```python
import jax
import jax.numpy as jnp
from jax import lax
from jax.sharding import PartitionSpec as P


def renorm(raw_weights, target):
    column_scale = target[:, None, :] * lax.rsqrt(
        jnp.sum(raw_weights * raw_weights, axis=1, keepdims=True) + 1e-06
    )
    return (raw_weights * column_scale).astype(jnp.bfloat16)


def advance(
    weights_in, weights_out, queries_seg, keys_seg, values_seg, rates_seg, norm_in, norm_out, gain
):
    rows_here = queries_seg.shape[0]
    heads_here = weights_in.shape[0]
    head_width = weights_in.shape[1]
    hidden_width = weights_out.shape[1]
    key_heads = keys_seg.reshape(rows_here, heads_here, head_width)
    pre_keys = jnp.einsum("thd,hde->hte", key_heads, weights_in, preferred_element_type=jnp.float32)
    first_half = pre_keys[..., :hidden_width]
    second_half = pre_keys[..., hidden_width:]
    sigmoid_first = jax.nn.sigmoid(first_half)
    activated = first_half * sigmoid_first
    hidden = (activated * second_half).astype(jnp.bfloat16)
    value_heads = values_seg.reshape(rows_here, heads_here, head_width).astype(jnp.float32)
    scaled = (value_heads * rates_seg.astype(jnp.float32)[:, :, None]).astype(jnp.bfloat16)
    grad_hidden = jnp.einsum(
        "the,hfe->htf", scaled, weights_out, preferred_element_type=jnp.float32
    )
    grad_first = (
        grad_hidden * second_half * sigmoid_first * (1.0 + first_half * (1.0 - sigmoid_first))
    )
    grad_second = grad_hidden * activated
    grad_pre = jnp.concatenate([grad_first, grad_second], axis=-1).astype(jnp.bfloat16)
    raw_in = weights_in.astype(jnp.float32) + jnp.einsum(
        "thd,hte->hde", key_heads, grad_pre, preferred_element_type=jnp.float32
    )
    raw_out = weights_out.astype(jnp.float32) + jnp.einsum(
        "htf,the->hfe", hidden, scaled, preferred_element_type=jnp.float32
    )
    new_in = renorm(raw_in, norm_in)
    new_out = renorm(raw_out, norm_out)
    query_heads = queries_seg.reshape(rows_here, heads_here, head_width)
    pre_queries = jnp.einsum(
        "thd,hde->hte", query_heads, new_in, preferred_element_type=jnp.float32
    )
    hidden_queries = (
        jax.nn.silu(pre_queries[..., :hidden_width]) * pre_queries[..., hidden_width:]
    ).astype(jnp.bfloat16)
    fast_out = jnp.einsum(
        "htf,hfe->the", hidden_queries, new_out, preferred_element_type=jnp.float32
    )
    normed = fast_out * lax.rsqrt(jnp.mean(fast_out * fast_out, axis=-1, keepdims=True) + 1e-05)
    normed = normed * gain.reshape(heads_here, head_width)
    return (
        new_in,
        new_out,
        normed.reshape(rows_here, heads_here * head_width).astype(jnp.bfloat16),
    )


def shards(queries, keys, values, step_sizes, starts, resets, init_in, init_out, gain, out_proj):
    frames = lax.axis_size("frame")
    position = lax.axis_index("frame")
    videos = queries.shape[0]
    rows_block = queries.shape[1]
    norm_in = jnp.sqrt(jnp.sum(jnp.square(init_in.astype(jnp.float32)), axis=1))
    norm_out = jnp.sqrt(jnp.sum(jnp.square(init_out.astype(jnp.float32)), axis=1))
    padding = ((0, frames - videos), (0, 0), (0, 0))
    moved_queries, moved_keys, moved_values, moved_rates = (
        lax.all_to_all(jnp.pad(queries, padding), "frame", split_axis=0, concat_axis=1, tiled=True),
        lax.all_to_all(jnp.pad(keys, padding), "frame", split_axis=0, concat_axis=1, tiled=True),
        lax.all_to_all(jnp.pad(values, padding), "frame", split_axis=0, concat_axis=1, tiled=True),
        lax.all_to_all(
            jnp.pad(step_sizes, padding), "frame", split_axis=0, concat_axis=1, tiled=True
        ),
    )
    video_here = jnp.minimum(position, videos - 1)
    first_block = starts[video_here]
    reset_flags = resets[video_here]

    def local_segment(seg_index, loop_state):
        state_in, state_out, collected = loop_state
        block_now = (first_block + seg_index) % frames
        first_row = block_now * rows_block
        queries_seg = lax.dynamic_slice_in_dim(moved_queries[0], first_row, rows_block, 0)
        keys_seg = lax.dynamic_slice_in_dim(moved_keys[0], first_row, rows_block, 0)
        values_seg = lax.dynamic_slice_in_dim(moved_values[0], first_row, rows_block, 0)
        rates_seg = lax.dynamic_slice_in_dim(moved_rates[0], first_row, rows_block, 0)
        restart = jnp.logical_or(seg_index == 0, reset_flags[seg_index] == 1)
        weights_in = jnp.where(restart, init_in, state_in)
        weights_out = jnp.where(restart, init_out, state_out)
        new_in, new_out, normed = advance(
            weights_in,
            weights_out,
            queries_seg,
            keys_seg,
            values_seg,
            rates_seg,
            norm_in,
            norm_out,
            gain,
        )
        collected = lax.dynamic_update_slice_in_dim(collected, normed, first_row, 0)
        return (new_in, new_out, collected)

    empty_rows = jnp.zeros((moved_queries.shape[1], moved_queries.shape[2]), jnp.bfloat16)
    _, _, own_rows = lax.fori_loop(0, frames, local_segment, (init_in, init_out, empty_rows))
    returned = lax.all_to_all(own_rows[None], "frame", split_axis=1, concat_axis=0, tiled=True)
    normed_all = returned[:videos]
    flat_rows = normed_all.reshape(videos * rows_block, normed_all.shape[2])
    partial_value = jnp.dot(flat_rows, out_proj, preferred_element_type=jnp.float32)
    mixed_out = lax.psum_scatter(
        partial_value.astype(jnp.bfloat16), "head", scatter_dimension=1, tiled=True
    ).astype(jnp.float32)
    return mixed_out.astype(jnp.bfloat16).reshape(videos, rows_block, mixed_out.shape[1])


def solution(mesh):
    return jax.shard_map(
        shards,
        mesh=mesh,
        in_specs=(
            P(None, "frame", "head"),
            P(None, "frame", "head"),
            P(None, "frame", "head"),
            P(None, "frame", "head"),
            P(),
            P(),
            P("head", None, None),
            P("head", None, None),
            P("head"),
            P("head", None),
        ),
        out_specs=P(None, "frame", "head"),
        check_vma=False,
    )
```

profile of v0, /device:TPU:0, one launch (start us, length us, event | category | flops | bytes accessed | tf_op | source)
XLA Modules:
  0.0 665.5 jit_solution(5543504575499884247)
XLA Ops:
  7.9 5.2 all-to-all-start.2
  13.1 4.1 pad.17
  17.8 4.6 all-to-all-start.3
  24.9 46.6 %all-to-all-done.3 = bf16[8,256,1024]{2,1,0:T(8,128)(2,1)} async-done(((bf16[8,256,1024]{2,1,0:T(8,128)(2,1)}), bf16[8,256,1024]{2,1,0:T(8,128)(2,1)}, u32[]{:S(2)}, u32[]{:S(2)}) %all-to-all-start.3) | async-done | bytes 4194336 | tf_op jit(solution)/shard_map/all_to_all | solution.py:74
  71.5 4.6 all-to-all-start
  78.5 46.7 %all-to-all-done = bf16[8,256,1024]{2,1,0:T(8,128)(2,1)} async-done(((bf16[8,256,1024]{2,1,0:T(8,128)(2,1)}), bf16[8,256,1024]{2,1,0:T(8,128)(2,1)}, u32[]{:S(2)}, u32[]{:S(2)}) %all-to-all-start) | async-done | bytes 4194336 | tf_op jit(solution)/shard_map/all_to_all | solution.py:75
  125.1 4.6 all-to-all-start.1
  134.6 44.3 %all-to-all-done.1 = bf16[8,256,1024]{2,1,0:T(8,128)(2,1)} async-done(((bf16[8,256,1024]{2,1,0:T(8,128)(2,1)}), bf16[8,256,1024]{2,1,0:T(8,128)(2,1)}, u32[]{:S(2)}, u32[]{:S(2)}) %all-to-all-start.1) | async-done | bytes 4194336 | tf_op jit(solution)/shard_map/all_to_all | solution.py:76
  181.3 158.4 %while.20 = (s32[]{:T(128)}, bf16[4,256,1024]{2,1,0:T(8,128)(2,1)S(1)}, bf16[4,512,256]{2,1,0:T(8,128)(2,1)}, bf16[2048,1024]{0,1:T(8,128)(2,1)}, s32[8]{0:T(128...) while((s32[]{:T(128)}, ...), condition=%wide.wide.region_6.7_spmd, body=%wide.wide.region_2.6_spmd.sunk | while | flops 2449480704 | bytes 95033920 | solution.py:111
  186.9 2.7 reshape.137
  208.1 2.7 reshape.137
  227.7 2.7 reshape.137
  247.3 2.7 reshape.137
  266.9 2.7 reshape.137
  306.1 2.7 reshape.137
  325.7 2.7 reshape.137
  339.7 20.5 %copy.42 = bf16[1,2048,1024]{2,0,1:T(2,128)(2,1)} copy(bf16[1,2048,1024]{1,2,0:T(8,128)(2,1)} %bitcast.69) | data formatting | bytes 8388608 | tf_op jit(solution)/shard_map/broadcast_in_dim | solution.py:112
  360.7 26.0 %reduce = bf16[2048,1024]{1,0:T(8,128)(2,1)} reduce(bf16[2048,1,1024]{2,1,0:T(2,128)(2,1)} %bitcast.67, bf16[]{:T(256)} %broadcast.99), dimensions={1}, to_apply=%bitcast.20.reduce_sub_computation | reduce | bytes 8388610
  386.7 7.8 %reshape.133 = bf16[8,2,131072]{2,1,0:T(2,128)(2,1)} reshape(bf16[2048,1024]{1,0:T(8,128)(2,1)} %reduce) | data formatting | bytes 8388608
  394.5 54.2 %all_to_all.60 = bf16[8,2,131072]{2,1,0:T(2,128)(2,1)} all-to-all(bf16[8,2,131072]{2,1,0:T(2,128)(2,1)} %reshape.133), channel_id=1, replica_groups=mesh['frame'=8,'head'=4] {'frame'}, dimensions={0} | all-to-all | bytes 8388608 | tf_op jit(solution)/shard_map/all_to_all | solution.py:112
  448.7 8.8 %reshape.134 = bf16[2048,1,1024]{2,1,0:T(2,128)(2,1)} reshape(bf16[8,2,131072]{2,1,0:T(2,128)(2,1)} %all_to_all.60) | data formatting | bytes 8388608
  457.4 5.1 copy.53
  462.7 17.2 %convolution_convert_fusion = bf16[1024,5120]{1,0:T(8,128)(2,1)} fusion(bf16[1024,1024]{1,0:T(8,128)(2,1)S(1)} %bitcast.71, bf16[1024,5120]{1,0:T(8,128)(2,1)} %param.21), kind=kOutput, calls=%fused_computation.36 | convolution fusion | flops 10742661120 | bytes 23068672 | tf_op jit(solution)/shard_map/dot_general | solution.py:115
  480.0 178.6 %reduce-scatter.2.cloned.1.call-done = bf16[1024,1280]{1,0:T(8,128)(2,1)} async-done(((bf16[1024,5120]{1,0:T(8,128)(2,1)}), bf16[1024,1280]{1,0:T(8,128)(2,1)}) %reduce-scatter.2.cloned.1.call-update) | async-done | bytes 2621456 | tf_op jit(solution)/shard_map/reduce_scatter | solution.py:116
  (275 shorter events, 142.7 us)
Async XLA Ops:
  6.5 128.0 %copy-start = (s32[4,8]{1,0:T(4,128)S(1)}, s32[4,8]{1,0:T(4,128)}, u32[]{:S(2)}) copy-start(s32[4,8]{1,0:T(4,128)} %param.17) | copy-start | bytes 388
  7.9 10.0 %all-to-all-start.2 = ((bf16[8,256,4]{1,2,0:T(4,128)(2,1)}), bf16[8,256,4]{1,2,0:T(4,128)(2,1)S(1)}, u32[]{:S(2)}, u32[]{:S(2)}) async-start(bf16[8,256,4]{1,2,0:T(4,128)(2,1)} %pad.16), calls=%async_computation.2 | async-start | bytes 32768 | tf_op jit(solution)/shard_map/all_to_all | solution.py:77
  17.1 5.3 copy-start.7
  17.8 53.7 %all-to-all-start.3 = ((bf16[8,256,1024]{2,1,0:T(8,128)(2,1)}), bf16[8,256,1024]{2,1,0:T(8,128)(2,1)}, u32[]{:S(2)}, u32[]{:S(2)}) async-start(bf16[8,256,1024]{2,1,0:T(8,128)(2,1)} %pad.17), calls=%async_computation.3 | async-start | bytes 8388608 | tf_op jit(solution)/shard_map/all_to_all | solution.py:74
  24.9 51.2 %copy-start.8 = (bf16[4,256,1024]{2,1,0:T(8,128)(2,1)S(1)}, bf16[4,256,1024]{2,1,0:T(8,128)(2,1)}, u32[]{:S(2)}) copy-start(bf16[4,256,1024]{2,1,0:T(8,128)(2,1)} %param.14) | copy-start | bytes 6291460
  71.5 53.7 %all-to-all-start = ((bf16[8,256,1024]{2,1,0:T(8,128)(2,1)}), bf16[8,256,1024]{2,1,0:T(8,128)(2,1)}, u32[]{:S(2)}, u32[]{:S(2)}) async-start(bf16[8,256,1024]{2,1,0:T(8,128)(2,1)} %pad.14), calls=%async_computation | async-start | bytes 8388608 | tf_op jit(solution)/shard_map/all_to_all | solution.py:75
  78.5 51.3 %copy-start.11 = (f32[1024]{0:T(1024)S(1)}, f32[1024]{0:T(1024)}, u32[]{:S(2)}) copy-start(f32[1024]{0:T(1024)} %param.20) | copy-start | bytes 12292
  78.5 51.3 %copy-start.5 = (bf16[4,512,256]{2,1,0:T(8,128)(2,1)S(1)}, bf16[4,512,256]{2,1,0:T(8,128)(2,1)}, u32[]{:S(2)}) copy-start(bf16[4,512,256]{2,1,0:T(8,128)(2,1)} %param.19) | copy-start | bytes 3145732
  125.1 53.7 %all-to-all-start.1 = ((bf16[8,256,1024]{2,1,0:T(8,128)(2,1)}), bf16[8,256,1024]{2,1,0:T(8,128)(2,1)}, u32[]{:S(2)}, u32[]{:S(2)}) async-start(bf16[8,256,1024]{2,1,0:T(8,128)(2,1)} %pad.15), calls=%async_computation.1 | async-start | bytes 8388608 | tf_op jit(solution)/shard_map/all_to_all | solution.py:76
  129.7 528.9 %reduce-scatter.2.cloned.1.call-start = ((), (), s32[]{:S(2)}) async-start(), calls=%async_computation.6 | async-start | bytes 13107200 | tf_op jit(solution)/shard_map/reduce_scatter | solution.py:116
  131.0 2.2 copy-start.2
  197.6 2.8 copy-start.10
  217.2 2.8 copy-start.10
  231.8 1.8 copy-start.9
  236.8 2.8 copy-start.10
  251.3 1.8 copy-start.9
  256.4 2.8 copy-start.10
  275.9 2.8 copy-start.10
  290.5 1.8 copy-start.9
  295.5 2.8 copy-start.10
  315.2 2.8 copy-start.10
  329.7 1.8 copy-start.9
  334.8 2.8 copy-start.10
  480.0 178.6 %copy-start.1 = (s32[4,8]{1,0:T(4,128)S(1)}, s32[4,8]{1,0:T(4,128)}, u32[]{:S(2)}) copy-start(s32[4,8]{1,0:T(4,128)} %param.17) | copy-start | bytes 388
  (29 other events, 38.4 us)
Sparse Core Ops, SparseCore 0:
  480.1 178.4 reduce-scatter.1
where the time goes:
time: 669 us; the launch traced here: 665 us
  waiting for transfers between devices  317 us (47%)
  local copies, waits for them, and re-layouts  122 us (18%)
  matrix products  68.7 us (10%)
  other arithmetic  59.4 us (9%)
  blocking collectives  54.2 us (8%)
  starting transfers between devices  19 us (3%)
  between operations  13.5 us (2%)
  loops' own time  11.9 us (2%)
    reduce_scatter x1, waiting for transfers between devices, shards(): lax.psum_scatter(partial_value.astype(jnp.bfloat16), 'head', scatter_dime...  179 us
    all_to_all x1, blocking collectives, shards(): lax.all_to_all(own_rows[None], 'frame', split_axis=1, concat_axis=0, tile...  54.2 us
    all_to_all x1, waiting for transfers between devices, shards(): lax.all_to_all(jnp.pad(keys, padding), 'frame', split_axis=0, concat_axis...  46.7 us
    all_to_all x1, waiting for transfers between devices, shards(): lax.all_to_all(jnp.pad(queries, padding), 'frame', split_axis=0, concat_a...  46.6 us
    all_to_all x1, waiting for transfers between devices, shards(): lax.all_to_all(jnp.pad(values, padding), 'frame', split_axis=0, concat_ax...  44.3 us
    unnamed x1, other arithmetic  26 us
    unnamed x22, local copies, waits for them, and re-layouts  25.5 us
    convert_element_type x8, local copies, waits for them, and re-layouts, advance(): values_seg.reshape(rows_here, heads_here, head_width).astype(jnp.float32)  21.3 us
  transfers between devices with their start and end apart: 5, of which 5 were waited for; matrix products, arithmetic and copies ran while one was open for 2% of the time, Pallas kernels for 0%

commit v1 on v0

--- a/solution.py
+++ b/solution.py
@@ -72,7 +72,15 @@
     padding = ((0, frames - videos), (0, 0), (0, 0))
     moved_queries, moved_keys, moved_values, moved_rates = (
         lax.all_to_all(jnp.pad(queries, padding), "frame", split_axis=0, concat_axis=1, tiled=True),
-        lax.all_to_all(jnp.pad(keys, padding), "frame", split_axis=0, concat_axis=1, tiled=True),
+        jnp.concatenate(
+            lax.all_to_all(
+                jnp.stack(jnp.split(jnp.pad(keys, padding), lax.axis_size("frame"), axis=0)),
+                "frame",
+                0,
+                0,
+            ),
+            axis=1,
+        ),
         lax.all_to_all(jnp.pad(values, padding), "frame", split_axis=0, concat_axis=1, tiled=True),
         lax.all_to_all(
             jnp.pad(step_sizes, padding), "frame", split_axis=0, concat_axis=1, tiled=True

time: 669 us -> 672 us (level)
  local copies, waits for them, and re-layouts: 122 us -> 139 us
  waiting for transfers between devices: 317 us -> 305 us
    while x80 -> x89, local copies, waits for them, and re-layouts: 10.6 us -> 41.2 us
    convert_element_type x8, local copies, waits for them, and re-layouts: 21.3 us -> 11.5 us  [advance(): values_seg.reshape(rows_here, heads_here, head_width).astype(jnp.float32)]
    dynamic_slice x16 -> x8, local copies, waits for them, and re-layouts: 10.3 us -> 0.63 us  [local_segment(): keys_seg = lax.dynamic_slice_in_dim(moved_keys[0], first_row, rows_block, 0)]
    all_to_all x1, waiting for transfers between devices: 44.3 us -> 37.5 us  [shards(): lax.all_to_all(jnp.pad(values, padding), 'frame', split_axis=0, concat_ax...]
    unnamed x22 -> x29, local copies, waits for them, and re-layouts: 25.5 us -> 31.1 us
  transfers between devices with their start and end apart: 5 -> 5, of which waited for: 5 -> 5; matrix products, arithmetic and copies ran while one was open for 2% -> 4% of each run, Pallas kernels for 0% -> 0%
where the time goes in v1:
time: 672 us; the launch traced here: 669 us
  waiting for transfers between devices  305 us (45%)
  local copies, waits for them, and re-layouts  139 us (21%)
  matrix products  68.7 us (10%)
  other arithmetic  58.9 us (9%)
  blocking collectives  53.6 us (8%)
  starting transfers between devices  18.9 us (3%)
  between operations  13.5 us (2%)
  loops' own time  11.9 us (2%)
    reduce_scatter x1, waiting for transfers between devices, shards(): lax.psum_scatter(partial_value.astype(jnp.bfloat16), 'head', scatter_dime...  178 us
    all_to_all x1, blocking collectives, shards(): lax.all_to_all(own_rows[None], 'frame', split_axis=1, concat_axis=0, tile...  53.6 us
    all_to_all x1, waiting for transfers between devices, shards(): lax.all_to_all(jnp.stack(jnp.split(jnp.pad(keys, padding), lax.axis_size(...  46.6 us
    all_to_all x1, waiting for transfers between devices, shards(): lax.all_to_all(jnp.pad(queries, padding), 'frame', split_axis=0, concat_a...  42.3 us
    all_to_all x1, waiting for transfers between devices, shards(): lax.all_to_all(jnp.pad(values, padding), 'frame', split_axis=0, concat_ax...  37.5 us
    while x88, local copies, waits for them, and re-layouts  34 us
    unnamed x29, local copies, waits for them, and re-layouts  31.1 us
    unnamed x1, other arithmetic  26 us
  transfers between devices with their start and end apart: 5, of which 5 were waited for; matrix products, arithmetic and copies ran while one was open for 4% of the time, Pallas kernels for 0%

profile of v1, /device:TPU:0, one launch (start us, length us, event | category | flops | bytes accessed | tf_op | source)
XLA Modules:
  0.0 668.9 jit_solution(2173781453467331539)
XLA Ops:
  7.9 5.2 all-to-all-start.2
  13.1 4.1 pad.14
  17.8 4.6 all-to-all-start.3
  29.2 42.3 %all-to-all-done.3 = bf16[8,256,1024]{2,1,0:T(8,128)(2,1)} async-done(((bf16[8,256,1024]{2,1,0:T(8,128)(2,1)}), bf16[8,256,1024]{2,1,0:T(8,128)(2,1)}, u32[]{:S(2)}, u32[]{:S(2)}) %all-to-all-start.3) | async-done | bytes 4194336 | tf_op jit(solution)/shard_map/all_to_all | solution.py:74
  71.5 4.6 all-to-all-start
  76.1 2.4 pad.12
  78.5 46.6 %all-to-all-done = bf16[8,1,256,1024]{3,2,1,0:T(8,128)(2,1)} async-done(((bf16[8,1,256,1024]{3,2,1,0:T(8,128)(2,1)}), bf16[8,1,256,1024]{3,2,1,0:T(8,128)(2,1)}, u32[]{:S(2)}, u32[]{:S(2)}) %all-to-all-start) | async-done | bytes 4194336 | tf_op jit(solution)/shard_map/all_to_all | solution.py:76
  125.1 4.6 all-to-all-start.1
  134.2 7.2 %copy.51 = bf16[8,1,256,1024]{2,0,3,1:T(8,128)(2,1)} copy(bf16[8,1,256,1024]{3,2,1,0:T(8,128)(2,1)} %all-to-all-done) | data formatting | bytes 8388608 | tf_op jit(solution)/shard_map/while | solution.py:119
  141.4 37.5 %all-to-all-done.1 = bf16[8,256,1024]{2,1,0:T(8,128)(2,1)} async-done(((bf16[8,256,1024]{2,1,0:T(8,128)(2,1)}), bf16[8,256,1024]{2,1,0:T(8,128)(2,1)}, u32[]{:S(2)}, u32[]{:S(2)}) %all-to-all-start.1) | async-done | bytes 4194336 | tf_op jit(solution)/shard_map/all_to_all | solution.py:84
  178.8 2.5 broadcast_in_dim.24
  181.3 163.6 %while.20 = (s32[]{:T(128)}, bf16[4,256,1024]{2,1,0:T(8,128)(2,1)S(1)}, bf16[4,512,256]{2,1,0:T(8,128)(2,1)}, bf16[2048,1024]{0,1:T(8,128)(2,1)}, s32[8]{0:T(128...) while((s32[]{:T(128)}, ...), condition=%wide.wide.region_6.7_spmd, body=%wide.wide.region_2.6_spmd.sunk | while | flops 2449480704 | bytes 117054000 | solution.py:119
  183.2 2.2 dynamic-slice_convert_fusion.3
  204.2 2.2 dynamic-slice_convert_fusion.3
  224.6 2.2 dynamic-slice_convert_fusion.3
  244.9 2.2 dynamic-slice_convert_fusion.3
  344.8 20.5 %copy.53 = bf16[1,2048,1024]{2,0,1:T(2,128)(2,1)} copy(bf16[1,2048,1024]{1,2,0:T(8,128)(2,1)} %bitcast.89) | data formatting | bytes 8388608 | tf_op jit(solution)/shard_map/broadcast_in_dim | solution.py:120
  365.9 26.0 %reduce = bf16[2048,1024]{1,0:T(8,128)(2,1)} reduce(bf16[2048,1,1024]{2,1,0:T(2,128)(2,1)} %bitcast.87, bf16[]{:T(256)} %broadcast.105), dimensions={1}, to_apply=%bitcast.32.reduce_sub_computation | reduce | bytes 8388610
  391.8 7.8 %reshape.128 = bf16[8,2,131072]{2,1,0:T(2,128)(2,1)} reshape(bf16[2048,1024]{1,0:T(8,128)(2,1)} %reduce) | data formatting | bytes 8388608
  399.6 53.6 %all_to_all.53 = bf16[8,2,131072]{2,1,0:T(2,128)(2,1)} all-to-all(bf16[8,2,131072]{2,1,0:T(2,128)(2,1)} %reshape.128), channel_id=1, replica_groups=mesh['frame'=8,'head'=4] {'frame'}, dimensions={0} | all-to-all | bytes 8388608 | tf_op jit(solution)/shard_map/all_to_all | solution.py:120
  453.2 8.8 %reshape.129 = bf16[2048,1,1024]{2,1,0:T(2,128)(2,1)} reshape(bf16[8,2,131072]{2,1,0:T(2,128)(2,1)} %all_to_all.53) | data formatting | bytes 8388608
  462.0 5.1 copy.62
  467.2 17.2 %convolution_convert_fusion = bf16[1024,5120]{1,0:T(8,128)(2,1)} fusion(bf16[1024,1024]{1,0:T(8,128)(2,1)S(1)} %bitcast.91, bf16[1024,5120]{1,0:T(8,128)(2,1)} %param.21), kind=kOutput, calls=%fused_computation.36 | convolution fusion | flops 10742661120 | bytes 23068672 | tf_op jit(solution)/shard_map/dot_general | solution.py:123
  484.5 177.5 %reduce-scatter.2.cloned.1.call-done = bf16[1024,1280]{1,0:T(8,128)(2,1)} async-done(((bf16[1024,5120]{1,0:T(8,128)(2,1)}), bf16[1024,1280]{1,0:T(8,128)(2,1)}) %reduce-scatter.2.cloned.1.call-update) | async-done | bytes 2621456 | tf_op jit(solution)/shard_map/reduce_scatter | solution.py:124
  (283 shorter events, 156.9 us)
Async XLA Ops:
  6.5 127.6 %copy-start = (s32[4,8]{1,0:T(4,128)S(1)}, s32[4,8]{1,0:T(4,128)}, u32[]{:S(2)}) copy-start(s32[4,8]{1,0:T(4,128)} %param.17) | copy-start | bytes 388
  7.9 10.0 %all-to-all-start.2 = ((bf16[8,256,4]{1,2,0:T(4,128)(2,1)}), bf16[8,256,4]{1,2,0:T(4,128)(2,1)S(1)}, u32[]{:S(2)}, u32[]{:S(2)}) async-start(bf16[8,256,4]{1,2,0:T(4,128)(2,1)} %pad.13), calls=%async_computation.2 | async-start | bytes 32768 | tf_op jit(solution)/shard_map/all_to_all | solution.py:85
  17.1 5.3 copy-start.8
  17.8 53.7 %all-to-all-start.3 = ((bf16[8,256,1024]{2,1,0:T(8,128)(2,1)}), bf16[8,256,1024]{2,1,0:T(8,128)(2,1)}, u32[]{:S(2)}, u32[]{:S(2)}) async-start(bf16[8,256,1024]{2,1,0:T(8,128)(2,1)} %pad.14), calls=%async_computation.3 | async-start | bytes 8388608 | tf_op jit(solution)/shard_map/all_to_all | solution.py:74
  29.2 46.8 %copy-start.7 = (bf16[4,256,1024]{2,1,0:T(8,128)(2,1)S(1)}, bf16[4,256,1024]{2,1,0:T(8,128)(2,1)}, u32[]{:S(2)}) copy-start(bf16[4,256,1024]{2,1,0:T(8,128)(2,1)} %param.14) | copy-start | bytes 6291460
  71.5 53.7 %all-to-all-start = ((bf16[8,1,256,1024]{3,2,1,0:T(8,128)(2,1)}), bf16[8,1,256,1024]{3,2,1,0:T(8,128)(2,1)}, u32[]{:S(2)}, u32[]{:S(2)}) async-start(bf16[8,1,256,1024]{3,2,1,0:T(8,128)(2,1)} %broadcast_dynamic-update-slice_fusion.3), calls=%async_computation | async-start | bytes 8388608 | tf_op jit(solution)/shard_map/all_to_all | solution.py:76
  78.5 51.3 %copy-start.11 = (f32[1024]{0:T(1024)S(1)}, f32[1024]{0:T(1024)}, u32[]{:S(2)}) copy-start(f32[1024]{0:T(1024)} %param.20) | copy-start | bytes 12292
  78.5 51.3 %copy-start.5 = (bf16[4,512,256]{2,1,0:T(8,128)(2,1)S(1)}, bf16[4,512,256]{2,1,0:T(8,128)(2,1)}, u32[]{:S(2)}) copy-start(bf16[4,512,256]{2,1,0:T(8,128)(2,1)} %param.19) | copy-start | bytes 3145732
  125.1 53.7 %all-to-all-start.1 = ((bf16[8,256,1024]{2,1,0:T(8,128)(2,1)}), bf16[8,256,1024]{2,1,0:T(8,128)(2,1)}, u32[]{:S(2)}, u32[]{:S(2)}) async-start(bf16[8,256,1024]{2,1,0:T(8,128)(2,1)} %pad.12), calls=%async_computation.1 | async-start | bytes 8388608 | tf_op jit(solution)/shard_map/all_to_all | solution.py:84
  129.7 532.3 %reduce-scatter.2.cloned.1.call-start = ((), (), s32[]{:S(2)}) async-start(), calls=%async_computation.6 | async-start | bytes 13107200 | tf_op jit(solution)/shard_map/reduce_scatter | solution.py:124
  130.8 2.2 copy-start.3
  131.0 2.5 copy-start.12
  188.1 2.8 copy-start.2
  197.6 2.6 copy-start.10
  209.1 2.2 copy-start.2
  217.9 2.6 copy-start.10
  238.3 2.6 copy-start.10
  258.7 2.6 copy-start.10
  270.1 2.2 copy-start.2
  279.0 2.6 copy-start.10
  299.4 2.6 copy-start.10
  319.8 2.6 copy-start.10
  340.1 2.6 copy-start.10
  484.5 177.6 %copy-start.1 = (s32[4,8]{1,0:T(4,128)S(1)}, s32[4,8]{1,0:T(4,128)}, u32[]{:S(2)}) copy-start(s32[4,8]{1,0:T(4,128)} %param.17) | copy-start | bytes 388
  (29 other events, 47.7 us)
Sparse Core Ops, SparseCore 0:
  484.6 177.3 reduce-scatter.1
